TPU v7x, 32 devices: a whole 2x2x4 slice. The times are simulated.
32 devices in a mesh: dom: 8 (over z, y), grp: 4 (over x, core).
Axes of the slice: x: 2, y: 2, z: 4, core: 2. Of those that a mesh axis runs over, the one named last changes fastest.
Arguments:
- nodes: bfloat16 [4, 4096, 128], P('grp', 'dom'), may hold values from -6 to 6
- edges: bfloat16 [4, 32, 128, 128], P('grp', 'dom'), may hold values from -6 to 6
- senders: int32 [4, 32, 128], P('grp', 'dom'), may hold values from 0 to 767
- receivers: int32 [4, 32, 128], P('grp', 'dom'), may hold values from 0 to 511
- block_count: int32 [4, 8], P('grp', 'dom'), may hold values from 1 to 4
- send_rows: int32 [4, 8, 2, 128], P('grp', 'dom'), may hold values from 0 to 511
- node_cot: bfloat16 [4, 4096, 128], P('grp', 'dom'), may hold values from -6 to 6
- edge_cot: bfloat16 [4, 32, 128, 128], P('grp', 'dom'), may hold values from -6 to 6
- edge_w1: bfloat16 [384, 128], replicated, may hold values from -0.3125 to 0.3125
- edge_b1: float32 [128], replicated, may hold values from -3 to 3
- edge_w2: bfloat16 [128, 128], replicated, may hold values from -0.5 to 0.5
- edge_b2: float32 [128], replicated, may hold values from -3 to 3
- edge_gain: float32 [128], replicated, may hold values from 0.5 to 1.5
- edge_shift: float32 [128], replicated, may hold values from -3 to 3
- node_w1: bfloat16 [256, 128], replicated, may hold values from -0.375 to 0.375
- node_b1: float32 [128], replicated, may hold values from -3 to 3
- node_w2: bfloat16 [128, 128], replicated, may hold values from -0.5 to 0.5
- node_b2: float32 [128], replicated, may hold values from -3 to 3
- node_gain: float32 [128], replicated, may hold values from 0.5 to 1.5
- node_shift: float32 [128], replicated, may hold values from -3 to 3
Outputs:
- node_out: bfloat16 [4, 4096, 128], P('grp', 'dom')
- edge_out: bfloat16 [4, 32, 128, 128], P('grp', 'dom')
- grad_node: bfloat16 [4, 4096, 128], P('grp', 'dom')
- grad_edge: bfloat16 [4, 32, 128, 128], P('grp', 'dom')
- weight_grads: float32 [115712], replicated
Inputs may be any that keep to these rules, and one draw needn't show every extreme that they name: `senders`: rows below 512 are the device's own nodes; row 512 + k holds the k-th row sent by the lower neighbouring partition, row 640 + k the k-th row sent by the upper one. `receivers`: receivers are own nodes of the device that holds the edge. `block_count`: A device's live blocks are its first ones; the rest are padding. send_rows[g, d, 0, :] are own rows of device d sent to device d - 1 of group g, send_rows[g, d, 1, :] those sent to device d + 1; they may repeat; lists toward no device are unused.
All inputs are finite; a program needn't handle non-finite values.
Results may differ from a plain program's by a relative error of at most 0.0054.
Values may be sent and summed in bfloat16 or wider, within the bound.
A program may use at most 64 MiB of HBM per device.

v0:
```python
import math
import jax
import jax.numpy as jnp
from jax import lax
from jax.sharding import PartitionSpec as P

EPSILON = 1e-05


def extended(value, sides, width):
    for axis, dim in sides:
        size, length = (lax.axis_size(axis), value.shape[dim])
        up = [(i, (i + 1) % size) for i in range(size - 1)]
        down = [(j, i) for i, j in up]
        last = lax.slice_in_dim(value, length - width, length, axis=dim)
        leading = lax.slice_in_dim(value, 0, width, axis=dim)
        before = lax.ppermute(last, axis, up)
        after = lax.ppermute(leading, axis, down)
        value = jnp.concatenate([before, value, after], axis=dim)
    return value


def norm_forward(pre_norm, norm_gain, norm_shift):
    average = jnp.mean(pre_norm, axis=-1, keepdims=True)
    centred = pre_norm - average
    variance = jnp.mean(centred * centred, axis=-1, keepdims=True)
    inverse = lax.rsqrt(variance + EPSILON)
    normed = centred * inverse
    return (normed * norm_gain + norm_shift, normed, inverse)


def norm_backward(grad_out, normed, inverse, norm_gain):
    scaled = grad_out * norm_gain
    return inverse * (
        scaled
        - jnp.mean(scaled, axis=-1, keepdims=True)
        - normed * jnp.mean(scaled * normed, axis=-1, keepdims=True)
    )


def silu_slope(pre_act):
    sigmoid = jax.nn.sigmoid(pre_act)
    return sigmoid * (1.0 + pre_act * (1.0 - sigmoid))


def row_product(left, right):
    return lax.dot_general(
        left, right, (((0,), (0,)), ((), ())), preferred_element_type=jnp.float32
    )


def mlp_forward(inputs, weights):
    w_first, b_first, w_second, b_second, norm_gain, norm_shift = weights
    first_pre = jnp.dot(inputs, w_first, preferred_element_type=jnp.float32) + b_first
    hidden = jax.nn.silu(first_pre).astype(jnp.bfloat16)
    second_pre = jnp.dot(hidden, w_second, preferred_element_type=jnp.float32) + b_second
    output, normed, inverse = norm_forward(second_pre, norm_gain, norm_shift)
    return (output, (first_pre, hidden, normed, inverse))


def mlp_backward(inputs, saved, grad_out, weights):
    w_first, b_first, w_second, b_second, norm_gain, norm_shift = weights
    first_pre, hidden, normed, inverse = saved
    grad_second = norm_backward(grad_out, normed, inverse, norm_gain)
    second_low = grad_second.astype(jnp.bfloat16)
    grad_hidden = jnp.dot(second_low, w_second.T, preferred_element_type=jnp.float32)
    grad_first = grad_hidden * silu_slope(first_pre)
    first_low = grad_first.astype(jnp.bfloat16)
    grad_inputs = jnp.dot(first_low, w_first.T, preferred_element_type=jnp.float32)
    grads = (
        row_product(inputs, first_low),
        jnp.sum(grad_first, axis=0),
        row_product(hidden, second_low),
        jnp.sum(grad_second, axis=0),
        jnp.sum(grad_out * normed, axis=0),
        jnp.sum(grad_out, axis=0),
    )
    return (grad_inputs, grads)


def shards(
    nodes,
    edges,
    senders,
    receivers,
    block_count,
    send_rows,
    node_cot,
    edge_cot,
    edge_w1,
    edge_b1,
    edge_w2,
    edge_b2,
    edge_gain,
    edge_shift,
    node_w1,
    node_b1,
    node_w2,
    node_b2,
    node_gain,
    node_shift,
):
    edge_weights = (edge_w1, edge_b1, edge_w2, edge_b2, edge_gain, edge_shift)
    node_weights = (node_w1, node_b1, node_w2, node_b2, node_gain, node_shift)
    own_nodes = nodes[0]
    node_rows, width = own_nodes.shape
    block_total = senders.shape[1]
    block_rows = senders.shape[2]
    edge_rows = block_total * block_rows
    flat_edges = edges[0].reshape(edge_rows, width)
    flat_send = senders[0].reshape(edge_rows)
    flat_recv = receivers[0].reshape(edge_rows)
    flat_cot = edge_cot[0].reshape(edge_rows, width)
    live_blocks = block_count[0, 0]
    row_lists = send_rows[0, 0]
    slot_count = row_lists.shape[1]
    outgoing = own_nodes[row_lists.reshape(-1)].reshape(2, slot_count, width)
    padded = extended(outgoing, (("dom", 0),), 1)
    from_lower, from_upper = (padded[0], padded[3])
    node_table = jnp.concatenate([own_nodes, from_lower, from_upper], axis=0)
    group_blocks = 4
    span = group_blocks * block_rows
    step_total = (live_blocks + group_blocks - 1) // group_blocks

    def edge_indices(offset):
        positions = offset + jnp.arange(span, dtype=jnp.int32)
        live_mask = (positions // block_rows < live_blocks).astype(jnp.float32)[:, None]
        return (flat_send, flat_recv, live_mask)

    def edge_inputs(send_part, recv_part):
        return jnp.concatenate([flat_edges, node_table[send_part], own_nodes[recv_part]], axis=1)

    stores = ()

    def forward_step(step_index, state_tuple):
        aggregate, edge_out, kept = state_tuple
        offset = step_index * span
        send_part, recv_part, live_mask = edge_indices(offset)
        inputs = edge_inputs(send_part, recv_part)
        message, saved = mlp_forward(inputs, edge_weights)
        live_message = message * live_mask
        aggregate = aggregate.at[recv_part].add(live_message)
        updated = (inputs[:, :width].astype(jnp.float32) + live_message).astype(jnp.bfloat16)
        edge_out = updated
        kept = tuple(
            (
                lax.dynamic_update_slice_in_dim(buffer, piece, offset, 0)
                for buffer, piece in zip(kept, (inputs,) + saved)
            )
        )
        return (aggregate, edge_out, kept)

    aggregate, edge_out, kept = lax.fori_loop(
        0,
        step_total,
        forward_step,
        (jnp.zeros((node_rows, width), jnp.float32), flat_edges, stores),
    )
    node_inputs = jnp.concatenate([own_nodes, aggregate.astype(jnp.bfloat16)], axis=1)
    update, node_saved = mlp_forward(node_inputs, node_weights)
    node_out = (own_nodes.astype(jnp.float32) + update).astype(jnp.bfloat16)
    node_grad = node_cot[0].astype(jnp.float32)
    grad_node_inputs, node_grads = mlp_backward(node_inputs, node_saved, node_grad, node_weights)
    grad_aggregate = grad_node_inputs[:, width:]

    def backward_step(step_index, state_tuple):
        table_grad, grad_edge, totals = state_tuple
        offset = step_index * span
        send_part, recv_part, live_mask = edge_indices(offset)
        inputs = edge_inputs(send_part, recv_part)
        unused_output, saved = mlp_forward(inputs, edge_weights)
        cot_part = flat_cot.astype(jnp.float32)
        grad_message = live_mask * (cot_part + grad_aggregate[recv_part])
        grad_inputs, step_grads = mlp_backward(inputs, saved, grad_message, edge_weights)
        new_grad = (cot_part + grad_inputs[:, :width]).astype(jnp.bfloat16)
        grad_edge = new_grad
        table_grad = table_grad.at[send_part].add(grad_inputs[:, width : 2 * width])
        table_grad = table_grad.at[recv_part].add(grad_inputs[:, 2 * width :])
        totals = tuple((total + piece for total, piece in zip(totals, step_grads)))
        return (table_grad, grad_edge, totals)

    zero_grads = tuple((jnp.zeros(piece.shape, jnp.float32) for piece in edge_weights))
    table_grad, grad_edge, edge_grads = lax.fori_loop(
        0,
        step_total,
        backward_step,
        (jnp.zeros((node_table.shape[0], width), jnp.float32), flat_cot, zero_grads),
    )
    halo_grad = table_grad[node_rows:].reshape(2, slot_count, width)
    padded_grad = extended(halo_grad.astype(jnp.bfloat16), (("dom", 0),), 1).astype(halo_grad.dtype)
    back_lower, back_upper = (padded_grad[0], padded_grad[3])
    returned = jnp.concatenate([back_lower, back_upper], axis=0)
    local_grad = node_grad + grad_node_inputs[:, :width] + table_grad[:node_rows]
    local_grad = local_grad.at[row_lists.reshape(-1)].add(returned)
    grad_node = local_grad.astype(jnp.bfloat16)
    flat_grads = jnp.concatenate([piece.reshape(-1) for piece in edge_grads + node_grads])
    summed = lax.psum(flat_grads, ("dom", "grp"))
    scale = 1.0 / math.sqrt(lax.axis_size("dom") * lax.axis_size("grp") * edge_rows)
    weight_grads = summed * scale
    return (
        node_out[None],
        edge_out.reshape(1, block_total, block_rows, width),
        grad_node[None],
        grad_edge.reshape(1, block_total, block_rows, width),
        weight_grads,
    )


def solution(mesh):
    return jax.shard_map(
        shards,
        mesh=mesh,
        in_specs=(
            P("grp", "dom", None),
            P("grp", "dom", None, None),
            P("grp", "dom", None),
            P("grp", "dom", None),
            P("grp", "dom"),
            P("grp", "dom", None, None),
            P("grp", "dom", None),
            P("grp", "dom", None, None),
            P(),
            P(),
            P(),
            P(),
            P(),
            P(),
            P(),
            P(),
            P(),
            P(),
            P(),
            P(),
        ),
        out_specs=(
            P("grp", "dom", None),
            P("grp", "dom", None, None),
            P("grp", "dom", None),
            P("grp", "dom", None, None),
            P(),
        ),
        check_vma=False,
    )
```

profile of v0, /device:TPU:0, one launch (start us, length us, event | category | flops | bytes accessed | tf_op | source)
XLA Modules:
  0.0 210.2 jit_solution(15320110725477557572)
XLA Ops:
  7.2 0.7 copy-done.20
  7.9 1.6 gather_fusion.1
  9.7 1.3 collective-permute-start.1
  11.1 5.7 %collective-permute-start = (bf16[1,128,128]{1,2,0:T(8,128)(2,1)S(1)}, bf16[1,128,128]{1,2,0:T(8,128)(2,1)S(1)}, u32[]{:S(2)}, u32[]{:S(2)}) collective-permute-start(bf16[1,128,128]{1,2,0:T(8,128)(2,1)S(1)} %bitcast.159), channel_id=1, source_target_pairs={{0,4},{4,8},{8,12},{12,16},{16,20},{20,24},{24,28},{1,5},{5,9},{9,... | collective-permute-start | bytes 98312 | tf_op jit(solution)/shard_map/ppermute | solution.py:17
  16.8 0.6 copy-done.13
  17.6 0.7 convert_reduce_fusion
  19.2 1.3 gather_fusion.3
  20.6 0.7 copy.88
  21.3 0.3 copy-done.2
  21.6 0.7 copy.79
  22.5 1.3 gather_fusion.2
  23.9 0.5 add_reduce_fusion
  24.7 0.6 copy-done.9
  25.3 5.3 %while.42 = (s32[]{:T(128)}, f32[512,128]{1,0:T(8,128)S(1)}, bf16[512,128]{1,0:T(8,128)(2,1)}, s32[]{:T(128)}, s32[512]{0:T(512)S(1)}, /*index=5*/f32[128]{0:T(1...) while((s32[]{:T(128)}, f32[512,128]{1,0:T(8,128)S(1)}, ...), condition=%wide.region_4.5_spmd, body=%wide.region_2.4_spmd.sunk | while | flops 1060867 | bytes 1078433 | solution.py:153
  25.3 0.7 fusion.116
  26.0 0.9 add_convert_fusion.3
  26.9 3.7 %scatter_custom_fusion.15 = f32[512,128]{1,0:T(8,128)S(1)} fusion(f32[512,128]{1,0:T(8,128)S(1)} %get-tuple-element.1141, s32[512]{0:T(512)S(1)} %bitcast.155, f32[512,128]{1,0:T(8,128)S(1)} %get-tuple-element.1161, f32[512]{0:T(512)S(1)} %fusion.116, f32[128]{0:T(128)S(1)} %get-tuple-element.1165, f32[128]{0:T(128)S(1)} %get-tuple-element.1164, ...), kind=kCustom, calls=%fused_computation.11.clone.1 | custom fusion | flops 458752 | bytes 531968 | tf_op jit(solution)/shard_map/while/body/scatter-add | solution.py:142
  30.7 0.5 copy-done.23
  31.3 0.3 convolution_add_fusion.5
  31.5 0.5 copy-done.24
  32.0 0.3 fusion.77
  32.3 0.6 copy-done.18
  33.1 0.9 convolution_bitcast_fusion.1
  34.1 0.8 fusion.78
  34.9 0.9 convolution_bitcast_fusion
  36.0 0.7 fusion.73
  36.7 1.0 gather_fusion.4
  37.9 0.5 broadcast.465.clone.2
  38.4 0.6 broadcast.465.clone.1
  39.0 0.5 broadcast.465.clone
  39.5 0.5 broadcast.465
  40.1 17.7 %while.43 = (s32[]{:T(128)}, f32[768,128]{1,0:T(8,128)S(1)}, bf16[512,128]{0,1:T(8,128)(2,1)}, f32[384,128]{1,0:T(8,128)S(1)}, f32[128]{0:T(128)}, /*index=5*/f3...) while((s32[]{:T(128)}, f32[768,128]{1,0:T(8,128)S(1)}, ...), condition=%wide.region_20.21_spmd, body=%wide.region_9.20_spmd.sunk | while | flops 204813824 | bytes 10293525 | solution.py:183
  40.3 0.7 fusion.130
  41.0 1.3 gather_fusion
  42.5 0.3 convolution_add_fusion.10
  42.7 0.3 fusion.129
  43.4 1.1 add.621
  44.5 1.3 add.622
  45.8 1.1 add.623
  46.9 0.3 convolution_add_fusion.12
  47.2 1.0 fusion.132
  48.2 0.3 convolution_add_fusion.11
  48.5 1.1 add.620
  50.1 0.7 fusion.134
  50.8 3.5 %scatter_custom_fusion.18 = f32[768,128]{1,0:T(8,128)S(1)} fusion(f32[768,128]{1,0:T(8,128)S(1)} %get-tuple-element.1196, s32[512]{0:T(512)S(1)} %bitcast.147, f32[512,384]{1,0:T(8,128)S(1)} %fusion.133), kind=kCustom, calls=%fused_computation.43.clone.1 | custom fusion | flops 65536 | bytes 655360 | tf_op jit(solution)/shard_map/while/body/scatter-add | solution.py:177
  54.3 3.5 %scatter_custom_fusion.19 = f32[768,128]{1,0:T(8,128)S(1)} fusion(f32[768,128]{1,0:T(8,128)S(1)} %scatter_custom_fusion.18, s32[512]{0:T(512)S(1)} %bitcast.154, f32[512,384]{1,0:T(8,128)S(1)} %fusion.133), kind=kCustom, calls=%fused_computation.41.clone.1 | custom fusion | flops 65536 | bytes 655360 | tf_op jit(solution)/shard_map/while/body/scatter-add | solution.py:178
  58.0 0.8 copy-done.4
  59.0 4.8 %collective-permute-start.2 = (bf16[1,128,128]{2,1,0:T(8,128)(2,1)S(1)}, bf16[1,128,128]{2,1,0:T(8,128)(2,1)S(1)}, u32[]{:S(2)}, u32[]{:S(2)}) collective-permute-start(bf16[1,128,128]{2,1,0:T(8,128)(2,1)S(1)} %get-tuple-element.858), channel_id=1, source_target_pairs={{0,4},{4,8},{8,12},{12,16},{16,20},{20,24},{24,28},{1,5},{5,9},{9,... | collective-permute-start | bytes 98312 | tf_op jit(solution)/shard_map/ppermute | solution.py:17
  63.8 1.3 collective-permute-start.3
  65.2 0.6 constant_dynamic-update-slice_fusion.12
  65.8 0.6 constant_dynamic-update-slice_fusion.11
  66.4 0.7 constant_dynamic-update-slice_fusion.10
  67.1 0.6 constant_dynamic-update-slice_fusion.9
  67.8 0.6 copy-done.28
  68.6 0.6 copy-done.19
  69.5 0.4 copy-done.22
  69.9 0.5 copy-done.7
  70.4 0.8 copy.61
  71.1 0.8 copy.62
  72.1 0.8 slice-done
  72.9 2.1 scatter_custom_fusion.3
  75.0 0.7 convert_bitcast_fusion.1
  75.6 125.9 %all-reduce.2.cloned.1.call-done = f32[115712]{0:T(1024)} async-done(((f32[115712]{0:T(1024)}), f32[115712]{0:T(1024)}) %all-reduce.2.cloned.1.call-update) | async-done | bytes 462864 | tf_op jit(solution)/shard_map/psum | solution.py:197
  201.5 1.8 broadcast_multiply_fusion.4
  (114 shorter events, 3.9 us)
Async XLA Ops:
  7.2 23.5 %copy-start = (bf16[256,128]{1,0:T(8,128)(2,1)S(1)}, bf16[256,128]{1,0:T(8,128)(2,1)}, u32[]{:S(2)}) copy-start(bf16[256,128]{1,0:T(8,128)(2,1)} %param.38) | copy-start | bytes 196612
  7.2 0.7 copy-start.20
  7.2 194.4 %all-reduce.2.cloned.1.call-start = ((), (), s32[]{:S(2)}) async-start(), calls=%async_computation | async-start | bytes 925696 | tf_op jit(solution)/shard_map/psum | solution.py:197
  9.6 7.9 %copy-start.10 = (bf16[1,512,128]{2,1,0:T(8,128)(2,1)S(1)}, bf16[1,512,128]{2,1,0:T(8,128)(2,1)}, u32[]{:S(2)}) copy-start(bf16[1,512,128]{2,1,0:T(8,128)(2,1)} %param.30) | copy-start | bytes 393220
  9.7 12.6 %collective-permute-start.1 = (bf16[1,128,128]{1,2,0:T(8,128)(2,1)S(1)}, bf16[1,128,128]{1,2,0:T(8,128)(2,1)S(1)}, u32[]{:S(2)}, u32[]{:S(2)}) collective-permute-start(bf16[1,128,128]{1,2,0:T(8,128)(2,1)S(1)} %bitcast.158), channel_id=1, source_target_pairs={{4,0},{8,4},{12,8},{16,12},{20,16},{24,20},{28,24},{5,1},{9,5},{13... | collective-permute-start | bytes 98312 | tf_op jit(solution)/shard_map/ppermute | solution.py:18
  11.1 5.7 %copy-start.8 = (s32[1,4,128]{2,1,0:T(4,128)S(1)}, s32[1,4,128]{2,1,0:T(4,128)}, u32[]{:S(2)}) copy-start(s32[1,4,128]{2,1,0:T(4,128)} %param.27) | copy-start | bytes 6148
  11.1 11.1 %collective-permute-start = (bf16[1,128,128]{1,2,0:T(8,128)(2,1)S(1)}, bf16[1,128,128]{1,2,0:T(8,128)(2,1)S(1)}, u32[]{:S(2)}, u32[]{:S(2)}) collective-permute-start(bf16[1,128,128]{1,2,0:T(8,128)(2,1)S(1)} %bitcast.159), channel_id=1, source_target_pairs={{0,4},{4,8},{8,12},{12,16},{16,20},{20,24},{24,28},{1,5},{5,9},{9,... | collective-permute-start | bytes 98312 | tf_op jit(solution)/shard_map/ppermute | solution.py:17
  16.8 0.7 copy-start.13
  17.6 1.4 copy-start.1
  19.1 1.4 copy-start.11
  20.6 1.0 copy-start.2
  22.4 1.4 copy-start.3
  22.4 1.4 copy-start.15
  22.5 1.4 copy-start.17
  22.5 1.4 copy-start.25
  24.6 0.7 copy-start.9
  24.6 0.7 copy-start.16
  30.6 0.7 copy-start.23
  31.2 0.8 copy-start.24
  31.3 0.8 copy-start.27
  32.3 0.7 copy-start.18
  54.3 3.5 %copy-start.26 = (bf16[128,128]{1,0:T(8,128)(2,1)S(1)}, bf16[128,128]{1,0:T(8,128)(2,1)}, u32[]{:S(2)}) copy-start(bf16[128,128]{1,0:T(8,128)(2,1)} %get-tuple-element.1286) | copy-start | bytes 98308 | tf_op jit(solution)/shard_map/while
  57.8 12.1 %copy-start.6 = (bf16[768,128]{1,0:T(8,128)(2,1)}, bf16[768,128]{1,0:T(8,128)(2,1)S(1)}, u32[]{:S(2)}) copy-start(bf16[768,128]{1,0:T(8,128)(2,1)S(1)} %convert.3) | copy-start | bytes 589828
  57.8 1.0 copy-start.4
  59.0 13.1 %collective-permute-start.2 = (bf16[1,128,128]{2,1,0:T(8,128)(2,1)S(1)}, bf16[1,128,128]{2,1,0:T(8,128)(2,1)S(1)}, u32[]{:S(2)}, u32[]{:S(2)}) collective-permute-start(bf16[1,128,128]{2,1,0:T(8,128)(2,1)S(1)} %get-tuple-element.858), channel_id=1, source_target_pairs={{0,4},{4,8},{8,12},{12,16},{16,20},{20,24},{24,28},{1,5},{5,9},{9,... | collective-permute-start | bytes 98312 | tf_op jit(solution)/shard_map/ppermute | solution.py:17
  63.8 8.3 %collective-permute-start.3 = (bf16[1,128,128]{2,1,0:T(8,128)(2,1)S(1)}, bf16[1,128,128]{2,1,0:T(8,128)(2,1)S(1)}, u32[]{:S(2)}, u32[]{:S(2)}) collective-permute-start(bf16[1,128,128]{2,1,0:T(8,128)(2,1)S(1)} %get-tuple-element.859), channel_id=1, source_target_pairs={{4,0},{8,4},{12,8},{16,12},{20,16},{24,20},{28,24},{5,1},{9,5},{13... | collective-permute-start | bytes 98312 | tf_op jit(solution)/shard_map/ppermute | solution.py:18
  65.1 2.6 %copy-start.12 = (f32[32768]{0:T(1024)S(1)}, f32[32768]{0:T(1024)}, u32[]{:S(2)}) copy-start(f32[32768]{0:T(1024)} %convolution_bitcast_fusion) | copy-start | bytes 393220
  67.7 0.8 copy-start.14
  67.8 0.6 copy-start.28
  68.6 0.7 copy-start.19
  68.6 0.7 copy-start.21
  69.2 0.7 copy-start.22
  69.5 0.9 copy-start.7
  69.9 2.1 %copy-start.5 = (f32[115712]{0:T(1024)}, f32[115712]{0:T(1024)S(1)}, u32[]{:S(2)}) copy-start(f32[115712]{0:T(1024)S(1)} %constant_dynamic-update-slice_fusion.3) | copy-start | bytes 1388548
  72.0 0.8 slice-start
Sparse Core Ops, SparseCore 0:
  72.2 129.3 all-reduce.1
where the time goes:
time: 211 us; the launch traced here: 210 us
  waiting for transfers between devices  126 us (60%)
  local copies, waits for them, and re-layouts  24.7 us (12%)
  other arithmetic  24.5 us (12%)
  between operations  15.3 us (7%)
  starting transfers between devices  13.1 us (6%)
  matrix products  6.24 us (3%)
    psum x1, waiting for transfers between devices, shards(): summed = lax.psum(flat_grads, ('dom', 'grp'))  126 us
    unnamed x75, local copies, waits for them, and re-layouts  12.4 us
    ppermute x2, starting transfers between devices, extended(): before = lax.ppermute(last, axis, up)  10.5 us
    add x4, other arithmetic, backward_step(): totals = tuple((total + piece for total, piece in zip(totals, step_grads)))  4.61 us
  transfers between devices with their start and end apart: 5, of which 1 were waited for; matrix products, arithmetic and copies ran while one was open for 5% of the time, Pallas kernels for 0%

commit v1 on v0

--- a/solution.py
+++ b/solution.py
@@ -194,7 +194,9 @@
     local_grad = local_grad.at[row_lists.reshape(-1)].add(returned)
     grad_node = local_grad.astype(jnp.bfloat16)
     flat_grads = jnp.concatenate([piece.reshape(-1) for piece in edge_grads + node_grads])
-    summed = lax.psum(flat_grads, ("dom", "grp"))
+    summed = flat_grads
+    for over in ("grp", "dom"):
+        summed = lax.psum(summed, over)
     scale = 1.0 / math.sqrt(lax.axis_size("dom") * lax.axis_size("grp") * edge_rows)
     weight_grads = summed * scale
     return (

time: 211 us -> 184 us (0.87)
  waiting for transfers between devices: 126 us -> 101 us
    psum x1 -> x2, waiting for transfers between devices: 126 us -> 98.6 us  [shards(): summed = lax.psum(summed, over)]
    ppermute x2, waiting for transfers between devices: 0.01 us -> 2.83 us  [extended(): after = lax.ppermute(leading, axis, down)]
  transfers between devices with their start and end apart: 5 -> 6, of which waited for: 1 -> 3; matrix products, arithmetic and copies ran while one was open for 5% -> 4% of each run, Pallas kernels for 0% -> 0%
where the time goes in v1:
time: 184 us; the launch traced here: 183 us
  waiting for transfers between devices  101 us (55%)
  other arithmetic  24.5 us (13%)
  local copies, waits for them, and re-layouts  23.5 us (13%)
  between operations  15.3 us (8%)
  starting transfers between devices  11.8 us (6%)
  matrix products  6.24 us (3%)
    psum x2, waiting for transfers between devices, shards(): summed = lax.psum(summed, over)  98.6 us
    unnamed x75, local copies, waits for them, and re-layouts  12.7 us
    ppermute x2, starting transfers between devices, extended(): before = lax.ppermute(last, axis, up)  9.18 us
    add x4, other arithmetic, backward_step(): totals = tuple((total + piece for total, piece in zip(totals, step_grads)))  4.61 us
  transfers between devices with their start and end apart: 6, of which 3 were waited for; matrix products, arithmetic and copies ran while one was open for 4% of the time, Pallas kernels for 0%

profile of v1, /device:TPU:0, one launch (start us, length us, event | category | flops | bytes accessed | tf_op | source)
XLA Modules:
  0.0 183.3 jit_solution(12328088851232060005)
XLA Ops:
  7.2 0.7 copy-done.20
  7.9 1.6 gather_fusion.1
  9.7 1.3 collective-permute-start.1
  11.1 5.7 %collective-permute-start = (bf16[1,128,128]{1,2,0:T(8,128)(2,1)S(1)}, bf16[1,128,128]{1,2,0:T(8,128)(2,1)S(1)}, u32[]{:S(2)}, u32[]{:S(2)}) collective-permute-start(bf16[1,128,128]{1,2,0:T(8,128)(2,1)S(1)} %bitcast.159), channel_id=1, source_target_pairs={{0,4},{4,8},{8,12},{12,16},{16,20},{20,24},{24,28},{1,5},{5,9},{9,... | collective-permute-start | bytes 98312 | tf_op jit(solution)/shard_map/ppermute | solution.py:17
  16.8 0.6 copy-done.13
  17.6 0.7 convert_reduce_fusion
  19.2 1.3 gather_fusion.3
  20.6 0.7 copy.88
  21.3 0.3 copy-done.2
  21.6 0.7 copy.79
  22.5 1.3 gather_fusion.2
  23.9 0.5 add_reduce_fusion
  24.7 0.6 copy-done.9
  25.3 5.3 %while.42 = (s32[]{:T(128)}, f32[512,128]{1,0:T(8,128)S(1)}, bf16[512,128]{1,0:T(8,128)(2,1)}, s32[]{:T(128)}, s32[512]{0:T(512)S(1)}, /*index=5*/f32[128]{0:T(1...) while((s32[]{:T(128)}, f32[512,128]{1,0:T(8,128)S(1)}, ...), condition=%wide.region_4.5_spmd, body=%wide.region_2.4_spmd.sunk | while | flops 1060867 | bytes 1078433 | solution.py:153
  25.3 0.7 fusion.116
  26.0 0.9 add_convert_fusion.3
  26.9 3.7 %scatter_custom_fusion.15 = f32[512,128]{1,0:T(8,128)S(1)} fusion(f32[512,128]{1,0:T(8,128)S(1)} %get-tuple-element.1141, s32[512]{0:T(512)S(1)} %bitcast.155, f32[512,128]{1,0:T(8,128)S(1)} %get-tuple-element.1161, f32[512]{0:T(512)S(1)} %fusion.116, f32[128]{0:T(128)S(1)} %get-tuple-element.1165, f32[128]{0:T(128)S(1)} %get-tuple-element.1164, ...), kind=kCustom, calls=%fused_computation.11.clone.1 | custom fusion | flops 458752 | bytes 531968 | tf_op jit(solution)/shard_map/while/body/scatter-add | solution.py:142
  30.7 0.5 copy-done.23
  31.3 0.3 convolution_add_fusion.5
  31.5 0.5 copy-done.24
  32.0 0.3 fusion.77
  32.3 0.6 copy-done.18
  33.1 0.9 convolution_bitcast_fusion.1
  34.1 0.8 fusion.78
  34.9 0.9 convolution_bitcast_fusion
  36.0 1.0 gather_fusion.4
  37.2 0.8 copy.69
  38.1 0.5 broadcast.465.clone.2
  38.6 0.6 broadcast.465.clone.1
  39.2 0.5 broadcast.465.clone
  39.7 0.5 broadcast.465
  40.2 17.7 %while.43 = (s32[]{:T(128)}, f32[768,128]{1,0:T(8,128)S(1)}, bf16[512,128]{0,1:T(8,128)(2,1)}, f32[384,128]{1,0:T(8,128)S(1)}, f32[128]{0:T(128)}, /*index=5*/f3...) while((s32[]{:T(128)}, f32[768,128]{1,0:T(8,128)S(1)}, ...), condition=%wide.region_20.21_spmd, body=%wide.region_9.20_spmd.sunk | while | flops 204813824 | bytes 10293525 | solution.py:183
  40.4 0.7 fusion.130
  41.1 1.3 gather_fusion
  42.6 0.3 convolution_add_fusion.10
  42.9 0.3 fusion.129
  43.6 1.1 add.623
  44.7 1.3 add.624
  46.0 1.1 add.625
  47.1 0.3 convolution_add_fusion.12
  47.3 1.0 fusion.132
  48.4 0.3 convolution_add_fusion.11
  48.7 1.1 add.622
  50.3 0.7 fusion.134
  50.9 3.5 %scatter_custom_fusion.18 = f32[768,128]{1,0:T(8,128)S(1)} fusion(f32[768,128]{1,0:T(8,128)S(1)} %get-tuple-element.1196, s32[512]{0:T(512)S(1)} %bitcast.147, f32[512,384]{1,0:T(8,128)S(1)} %fusion.133), kind=kCustom, calls=%fused_computation.43.clone.1 | custom fusion | flops 65536 | bytes 655360 | tf_op jit(solution)/shard_map/while/body/scatter-add | solution.py:177
  54.4 3.5 %scatter_custom_fusion.19 = f32[768,128]{1,0:T(8,128)S(1)} fusion(f32[768,128]{1,0:T(8,128)S(1)} %scatter_custom_fusion.18, s32[512]{0:T(512)S(1)} %bitcast.154, f32[512,384]{1,0:T(8,128)S(1)} %fusion.133), kind=kCustom, calls=%fused_computation.41.clone.1 | custom fusion | flops 65536 | bytes 655360 | tf_op jit(solution)/shard_map/while/body/scatter-add | solution.py:178
  58.1 0.6 constant_dynamic-update-slice_fusion.12
  58.8 0.6 constant_dynamic-update-slice_fusion.11
  59.5 0.7 constant_dynamic-update-slice_fusion.10
  60.1 0.6 constant_dynamic-update-slice_fusion.9
  60.8 0.6 copy-done.28
  61.5 0.6 copy-done.19
  62.3 0.7 copy-done.22
  63.0 0.8 copy-done.5
  63.9 34.6 %all-reduce.3.cloned.1.call-done = f32[115712]{0:T(1024)} async-done(((f32[115712]{0:T(1024)}), f32[115712]{0:T(1024)}) %all-reduce.3.cloned.1.call-update) | async-done | bytes 462864 | tf_op jit(solution)/shard_map/psum | solution.py:199
  98.5 3.5 %collective-permute-start.2 = (bf16[1,128,128]{2,1,0:T(8,128)(2,1)S(1)}, bf16[1,128,128]{2,1,0:T(8,128)(2,1)S(1)}, u32[]{:S(2)}, u32[]{:S(2)}) collective-permute-start(bf16[1,128,128]{2,1,0:T(8,128)(2,1)S(1)} %get-tuple-element.858), channel_id=1, source_target_pairs={{0,4},{4,8},{8,12},{12,16},{16,20},{20,24},{24,28},{1,5},{5,9},{9,... | collective-permute-start | bytes 98312 | tf_op jit(solution)/shard_map/ppermute | solution.py:17
  102.0 1.3 collective-permute-start.3
  103.3 0.8 copy.61
  104.1 0.8 copy.62
  105.0 2.8 %collective-permute-done.3 = bf16[1,128,128]{2,1,0:T(8,128)(2,1)S(1)} collective-permute-done((bf16[1,128,128]{2,1,0:T(8,128)(2,1)S(1)}, bf16[1,128,128]{2,1,0:T(8,128)(2,1)S(1)}, u32[]{:S(2)}, u32[]{:S(2)}) %collective-permute-start.3) | collective-permute-done | bytes 32800 | tf_op jit(solution)/shard_map/ppermute | solution.py:18
  107.9 2.1 %scatter_custom_fusion.3 = f32[512,128]{1,0:T(8,128)S(1)} fusion(f32[512,128]{1,0:T(8,128)S(1)} %copy.60, s32[256]{0:T(256)S(1)} %bitcast.163, f32[128,128]{1,0:T(8,128)S(1)} %get-tuple-element.862, f32[]{:T(128)} %constant.240, f32[128,128]{1,0:T(8,128)S(1)} %get-tuple-element.861), kind=kCustom, calls=%fused_computation.117 | custom fusion | flops 65536 | bytes 393220 | tf_op jit(solution)/shard_map/scatter-add | solution.py:194
  109.9 0.7 convert_bitcast_fusion.1
  110.6 64.0 %all-reduce.5.cloned.1.call-done = f32[115712]{0:T(1024)} async-done(((f32[115712]{0:T(1024)}), f32[115712]{0:T(1024)}) %all-reduce.5.cloned.1.call-update) | async-done | bytes 462864 | tf_op jit(solution)/shard_map/psum | solution.py:199
  174.6 1.8 broadcast_multiply_fusion.4
  (117 shorter events, 3.7 us)
Async XLA Ops:
  7.2 23.5 %copy-start = (bf16[256,128]{1,0:T(8,128)(2,1)S(1)}, bf16[256,128]{1,0:T(8,128)(2,1)}, u32[]{:S(2)}) copy-start(bf16[256,128]{1,0:T(8,128)(2,1)} %param.38) | copy-start | bytes 196612
  7.2 0.7 copy-start.20
  7.2 91.3 %all-reduce.3.cloned.1.call-start = ((), (), s32[]{:S(2)}) async-start(), calls=%async_computation | async-start | bytes 925696 | tf_op jit(solution)/shard_map/psum | solution.py:199
  9.6 7.9 %copy-start.10 = (bf16[1,512,128]{2,1,0:T(8,128)(2,1)S(1)}, bf16[1,512,128]{2,1,0:T(8,128)(2,1)}, u32[]{:S(2)}) copy-start(bf16[1,512,128]{2,1,0:T(8,128)(2,1)} %param.30) | copy-start | bytes 393220
  9.7 12.6 %collective-permute-start.1 = (bf16[1,128,128]{1,2,0:T(8,128)(2,1)S(1)}, bf16[1,128,128]{1,2,0:T(8,128)(2,1)S(1)}, u32[]{:S(2)}, u32[]{:S(2)}) collective-permute-start(bf16[1,128,128]{1,2,0:T(8,128)(2,1)S(1)} %bitcast.158), channel_id=1, source_target_pairs={{4,0},{8,4},{12,8},{16,12},{20,16},{24,20},{28,24},{5,1},{9,5},{13... | collective-permute-start | bytes 98312 | tf_op jit(solution)/shard_map/ppermute | solution.py:18
  11.1 5.7 %copy-start.8 = (s32[1,4,128]{2,1,0:T(4,128)S(1)}, s32[1,4,128]{2,1,0:T(4,128)}, u32[]{:S(2)}) copy-start(s32[1,4,128]{2,1,0:T(4,128)} %param.27) | copy-start | bytes 6148
  11.1 11.1 %collective-permute-start = (bf16[1,128,128]{1,2,0:T(8,128)(2,1)S(1)}, bf16[1,128,128]{1,2,0:T(8,128)(2,1)S(1)}, u32[]{:S(2)}, u32[]{:S(2)}) collective-permute-start(bf16[1,128,128]{1,2,0:T(8,128)(2,1)S(1)} %bitcast.159), channel_id=1, source_target_pairs={{0,4},{4,8},{8,12},{12,16},{16,20},{20,24},{24,28},{1,5},{5,9},{9,... | collective-permute-start | bytes 98312 | tf_op jit(solution)/shard_map/ppermute | solution.py:17
  16.8 0.7 copy-start.13
  17.6 1.4 copy-start.1
  19.1 1.4 copy-start.11
  20.6 1.0 copy-start.2
  22.4 1.4 copy-start.3
  22.4 1.4 copy-start.15
  22.5 1.4 copy-start.17
  22.5 1.4 copy-start.25
  24.6 0.7 copy-start.9
  24.6 0.7 copy-start.16
  30.6 0.7 copy-start.23
  31.2 0.8 copy-start.24
  31.3 0.8 copy-start.27
  32.3 0.7 copy-start.18
  54.4 3.5 %copy-start.26 = (bf16[128,128]{1,0:T(8,128)(2,1)S(1)}, bf16[128,128]{1,0:T(8,128)(2,1)}, u32[]{:S(2)}) copy-start(bf16[128,128]{1,0:T(8,128)(2,1)} %get-tuple-element.1290) | copy-start | bytes 98308 | tf_op jit(solution)/shard_map/while
  58.1 3.3 %copy-start.14 = (f32[16384]{0:T(1024)S(1)}, f32[16384]{0:T(1024)}, u32[]{:S(2)}) copy-start(f32[16384]{0:T(1024)} %convolution_bitcast_fusion.1) | copy-start | bytes 196612
  58.1 2.6 %copy-start.12 = (f32[32768]{0:T(1024)S(1)}, f32[32768]{0:T(1024)}, u32[]{:S(2)}) copy-start(f32[32768]{0:T(1024)} %convolution_bitcast_fusion) | copy-start | bytes 393220
  58.8 2.7 %copy-start.4 = (f32[512,128]{0,1:T(8,128)S(1)}, f32[512,128]{0,1:T(8,128)}, u32[]{:S(2)}) copy-start(f32[512,128]{0,1:T(8,128)} %copy.69) | copy-start | bytes 786436
  60.8 0.6 copy-start.28
  61.4 0.7 copy-start.19
  61.4 0.7 copy-start.21
  62.3 0.7 copy-start.22
  63.0 0.8 copy-start.5
  63.8 110.8 %all-reduce.5.cloned.1.call-start = ((), (), s32[]{:S(2)}) async-start(), calls=%async_computation.1 | async-start | bytes 925696 | tf_op jit(solution)/shard_map/psum | solution.py:199
  63.9 39.5 %copy-start.6 = (bf16[768,128]{1,0:T(8,128)(2,1)}, bf16[768,128]{1,0:T(8,128)(2,1)S(1)}, u32[]{:S(2)}) copy-start(bf16[768,128]{1,0:T(8,128)(2,1)S(1)} %convert.3) | copy-start | bytes 589828
  98.5 4.9 %copy-start.7 = (bf16[512,128]{0,1:T(8,128)(2,1)S(1)}, bf16[512,128]{0,1:T(8,128)(2,1)}, u32[]{:S(2)}) copy-start(bf16[512,128]{0,1:T(8,128)(2,1)} %get-tuple-element.1267) | copy-start | bytes 393220
  98.5 6.5 %collective-permute-start.2 = (bf16[1,128,128]{2,1,0:T(8,128)(2,1)S(1)}, bf16[1,128,128]{2,1,0:T(8,128)(2,1)S(1)}, u32[]{:S(2)}, u32[]{:S(2)}) collective-permute-start(bf16[1,128,128]{2,1,0:T(8,128)(2,1)S(1)} %get-tuple-element.858), channel_id=1, source_target_pairs={{0,4},{4,8},{8,12},{12,16},{16,20},{20,24},{24,28},{1,5},{5,9},{9,... | collective-permute-start | bytes 98312 | tf_op jit(solution)/shard_map/ppermute | solution.py:17
  102.0 5.8 %collective-permute-start.3 = (bf16[1,128,128]{2,1,0:T(8,128)(2,1)S(1)}, bf16[1,128,128]{2,1,0:T(8,128)(2,1)S(1)}, u32[]{:S(2)}, u32[]{:S(2)}) collective-permute-start(bf16[1,128,128]{2,1,0:T(8,128)(2,1)S(1)} %get-tuple-element.859), channel_id=1, source_target_pairs={{4,0},{8,4},{12,8},{16,12},{20,16},{24,20},{28,24},{5,1},{9,5},{13... | collective-permute-start | bytes 98312 | tf_op jit(solution)/shard_map/ppermute | solution.py:18
  104.9 3.0 %slice-start = ((bf16[768,128]{1,0:T(8,128)(2,1)}), bf16[256,128]{1,0:T(8,128)(2,1)S(1)}, s32[]{:S(2)}) async-start(bf16[768,128]{1,0:T(8,128)(2,1)} %copy-done.6), calls=%async_computation.2 | async-start | bytes 131072 | tf_op jit(solution)/shard_map/slice | solution.py:189
Sparse Core Ops, SparseCore 0:
  63.9 34.4 all-reduce.2
  101.9 72.7 all-reduce.4
